TPU v7x, 256 devices: a whole 4x4x8 slice. The times are simulated.
256 devices in a mesh: slab: 32 (over x, z), hodlr: 8 (over y, core).
Axes of the slice: x: 4, y: 4, z: 8, core: 2. Of those that a mesh axis runs over, the one named last changes fastest.
Arguments:
- sources: bfloat16 [32, 32, 16384], P('slab', None, 'hodlr'), may hold values from -2 to 2
- leaves: bfloat16 [32, 16, 1024, 1024], P('slab', 'hodlr'), may hold values from -1 to 2
- v_rows: bfloat16 [32, 4, 64, 16384], P('slab', None, None, 'hodlr'), may hold values from -0.0625 to 0.0625
- u_rows: bfloat16 [32, 4, 64, 16384], P('slab', None, None, 'hodlr'), may hold values from -0.1875 to 0.1875
Outputs:
- fronts: bfloat16 [32, 32, 16384], P('slab', None, 'hodlr')
All inputs are finite; a program needn't handle non-finite values.
Results may differ from a plain program's by a relative error of at most 0.025.
Values may be sent and summed in bfloat16 or wider, within the bound.
A program may use at most 64 MiB of HBM per device.

v0:
```python
import jax
import jax.numpy as jnp
from jax import lax
from jax.sharding import PartitionSpec as P


def passed_along(block, axis, distance):
    devices = range(lax.axis_size(axis))
    route = [(i - distance, i) for i in devices if i - distance in devices]
    return lax.ppermute(block, axis, route)


def local(sources, leaves, v_rows, u_rows):
    devices = lax.axis_size("hodlr")
    chain = lax.axis_size("slab")
    position = lax.axis_index("slab")
    member = lax.axis_index("hodlr")
    cross = devices.bit_length() - 1
    source = sources[0]
    leaf = leaves[0]
    right = v_rows[0]
    left = u_rows[0]
    shot_batch, width = source.shape
    rank = right.shape[1]
    nleaf = leaf.shape[0]
    leaf_size = leaf.shape[1]
    peers = jnp.arange(devices, dtype=jnp.int32)
    sibling_rows = []
    for tree_level in range(1, cross + 1):
        group = devices >> tree_level
        sibling_rows.append(
            (peers // group == jnp.bitwise_xor(member // group, 1)).astype(jnp.float32)
        )
    sibling_mask = jnp.stack(sibling_rows)

    def partials_of(w, factors):
        rows = w.shape[0]
        return jnp.einsum("sn,crn->csr", w, factors, preferred_element_type=jnp.float32).reshape(
            cross, rows * rank
        )

    def combine_gathered(gathered, rows):
        sibling = jnp.einsum("pcx,cp->cx", gathered, sibling_mask, precision=lax.Precision.HIGHEST)
        return sibling.reshape(cross, rows, rank).astype(jnp.bfloat16)

    def local_part(w):
        rows = w.shape[0]
        sweep_output = jnp.einsum(
            "sbj,bjo->sbo",
            w.reshape(rows, nleaf, leaf_size),
            leaf,
            preferred_element_type=jnp.float32,
        ).reshape(rows, width)
        block_size = width * devices >> 4
        block_list = width // block_size
        projection_rows = jnp.einsum(
            "kqc,vqc->kqv",
            w.reshape(rows, block_list, block_size),
            right[3].reshape(rank, block_list, block_size),
            preferred_element_type=jnp.float32,
        ).astype(jnp.bfloat16)
        swapped_halves = projection_rows.reshape(rows, block_list // 2, 2, rank)[
            :, :, ::-1
        ].reshape(rows, block_list, rank)
        sweep_output = sweep_output + jnp.einsum(
            "cwp,pwi->cwi",
            swapped_halves,
            left[3].reshape(rank, block_list, block_size),
            preferred_element_type=jnp.float32,
        ).reshape(rows, width)
        return sweep_output

    def finish(sweep_output, sibling):
        sweep_output = sweep_output + jnp.einsum(
            "csr,crn->sn", sibling, left[:cross], preferred_element_type=jnp.float32
        )
        return sweep_output.astype(jnp.bfloat16)

    def apply(w):
        rows = w.shape[0]
        partial_value = partials_of(w, right[:cross])
        sweep_output = local_part(w)
        gathered = lax.all_gather(partial_value[None], "hodlr", axis=0, tiled=True)
        sibling = combine_gathered(gathered, rows)
        return finish(sweep_output, sibling)

    groups = 1
    batch = shot_batch // groups

    def advance(step, carry):
        front, swept = carry
        incoming = passed_along(front, "slab", 1)
        offset = step - position
        valid = (offset >= 0) & (offset < groups)
        w = (source.astype(jnp.float32) + incoming.astype(jnp.float32)).astype(jnp.bfloat16)
        sweep_output = apply(w)
        current = swept
        swept = jnp.where(valid, sweep_output, current)
        return (sweep_output, swept)

    initial = (
        jnp.zeros((batch, width), jnp.bfloat16),
        jnp.zeros((shot_batch, width), jnp.bfloat16),
    )
    _, swept = lax.fori_loop(0, chain + groups - 1, advance, initial)
    return swept[None]


def solution(mesh):
    in_specs = (
        P("slab", None, "hodlr"),
        P("slab", "hodlr", None, None),
        P("slab", None, None, "hodlr"),
        P("slab", None, None, "hodlr"),
    )
    out_specs = P("slab", None, "hodlr")
    return jax.shard_map(local, mesh=mesh, in_specs=in_specs, out_specs=out_specs, check_vma=False)
```

profile of v0, /device:TPU:7, one launch (start us, length us, event | category | flops | bytes accessed | tf_op | source)
XLA Modules:
  0.0 952.1 jit_solution(5715799266085852439)
XLA Ops:
  0.1 951.3 %while.16 = (s32[]{:T(128)}, bf16[32,2048]{1,0:T(8,128)(2,1)S(1)}, bf16[32,2048]{1,0:T(8,128)(2,1)S(1)}, bf16[32,2048]{1,0:T(8,128)(2,1)}, bf16[2,1024,1024]{2,1...) while((s32[]{:T(128)}, bf16[32,2048]{1,0:T(8,128)(2,1)S(1)}, ...), condition=%wide.region_1.2_spmd.clone, body=%wide.region_0.1_spmd.clone.sunk | while | flops 202575872 | bytes 16732478 | solution.py:105
  6.0 5.1 collective-permute-done
  17.2 14.4 %all_gather.9 = f32[8,3,2048]{2,1,0:T(4,128)S(1)} all-gather(f32[1,3,2048]{2,1,0:T(4,128)S(1)} %reshape.133), channel_id=1, replica_groups=mesh['slab'=32,'hodlr'=8] {'hodlr'}, dimensions={0}, use_global_device_ids=true | all-gather | bytes 221184 | tf_op jit(solution)/shard_map/while/body/eval_jaxpr/all_gather | solution.py:83
  36.8 4.6 collective-permute-done
  47.6 13.7 %all_gather.9 = f32[8,3,2048]{2,1,0:T(4,128)S(1)} all-gather(f32[1,3,2048]{2,1,0:T(4,128)S(1)} %reshape.133), channel_id=1, replica_groups=mesh['slab'=32,'hodlr'=8] {'hodlr'}, dimensions={0}, use_global_device_ids=true | all-gather | bytes 221184 | tf_op jit(solution)/shard_map/while/body/eval_jaxpr/all_gather | solution.py:83
  66.4 4.6 collective-permute-done
  77.2 13.7 %all_gather.9 = f32[8,3,2048]{2,1,0:T(4,128)S(1)} all-gather(f32[1,3,2048]{2,1,0:T(4,128)S(1)} %reshape.133), channel_id=1, replica_groups=mesh['slab'=32,'hodlr'=8] {'hodlr'}, dimensions={0}, use_global_device_ids=true | all-gather | bytes 221184 | tf_op jit(solution)/shard_map/while/body/eval_jaxpr/all_gather | solution.py:83
  106.9 13.7 %all_gather.9 = f32[8,3,2048]{2,1,0:T(4,128)S(1)} all-gather(f32[1,3,2048]{2,1,0:T(4,128)S(1)} %reshape.133), channel_id=1, replica_groups=mesh['slab'=32,'hodlr'=8] {'hodlr'}, dimensions={0}, use_global_device_ids=true | all-gather | bytes 221184 | tf_op jit(solution)/shard_map/while/body/eval_jaxpr/all_gather | solution.py:83
  136.5 13.7 %all_gather.9 = f32[8,3,2048]{2,1,0:T(4,128)S(1)} all-gather(f32[1,3,2048]{2,1,0:T(4,128)S(1)} %reshape.133), channel_id=1, replica_groups=mesh['slab'=32,'hodlr'=8] {'hodlr'}, dimensions={0}, use_global_device_ids=true | all-gather | bytes 221184 | tf_op jit(solution)/shard_map/while/body/eval_jaxpr/all_gather | solution.py:83
  155.4 4.6 collective-permute-done
  166.2 13.7 %all_gather.9 = f32[8,3,2048]{2,1,0:T(4,128)S(1)} all-gather(f32[1,3,2048]{2,1,0:T(4,128)S(1)} %reshape.133), channel_id=1, replica_groups=mesh['slab'=32,'hodlr'=8] {'hodlr'}, dimensions={0}, use_global_device_ids=true | all-gather | bytes 221184 | tf_op jit(solution)/shard_map/while/body/eval_jaxpr/all_gather | solution.py:83
  185.0 4.6 collective-permute-done
  195.8 13.7 %all_gather.9 = f32[8,3,2048]{2,1,0:T(4,128)S(1)} all-gather(f32[1,3,2048]{2,1,0:T(4,128)S(1)} %reshape.133), channel_id=1, replica_groups=mesh['slab'=32,'hodlr'=8] {'hodlr'}, dimensions={0}, use_global_device_ids=true | all-gather | bytes 221184 | tf_op jit(solution)/shard_map/while/body/eval_jaxpr/all_gather | solution.py:83
  225.4 13.7 %all_gather.9 = f32[8,3,2048]{2,1,0:T(4,128)S(1)} all-gather(f32[1,3,2048]{2,1,0:T(4,128)S(1)} %reshape.133), channel_id=1, replica_groups=mesh['slab'=32,'hodlr'=8] {'hodlr'}, dimensions={0}, use_global_device_ids=true | all-gather | bytes 221184 | tf_op jit(solution)/shard_map/while/body/eval_jaxpr/all_gather | solution.py:83
  255.1 13.7 %all_gather.9 = f32[8,3,2048]{2,1,0:T(4,128)S(1)} all-gather(f32[1,3,2048]{2,1,0:T(4,128)S(1)} %reshape.133), channel_id=1, replica_groups=mesh['slab'=32,'hodlr'=8] {'hodlr'}, dimensions={0}, use_global_device_ids=true | all-gather | bytes 221184 | tf_op jit(solution)/shard_map/while/body/eval_jaxpr/all_gather | solution.py:83
  273.9 4.6 collective-permute-done
  284.7 13.7 %all_gather.9 = f32[8,3,2048]{2,1,0:T(4,128)S(1)} all-gather(f32[1,3,2048]{2,1,0:T(4,128)S(1)} %reshape.133), channel_id=1, replica_groups=mesh['slab'=32,'hodlr'=8] {'hodlr'}, dimensions={0}, use_global_device_ids=true | all-gather | bytes 221184 | tf_op jit(solution)/shard_map/while/body/eval_jaxpr/all_gather | solution.py:83
  303.6 4.6 collective-permute-done
  314.4 13.7 %all_gather.9 = f32[8,3,2048]{2,1,0:T(4,128)S(1)} all-gather(f32[1,3,2048]{2,1,0:T(4,128)S(1)} %reshape.133), channel_id=1, replica_groups=mesh['slab'=32,'hodlr'=8] {'hodlr'}, dimensions={0}, use_global_device_ids=true | all-gather | bytes 221184 | tf_op jit(solution)/shard_map/while/body/eval_jaxpr/all_gather | solution.py:83
  344.0 13.7 %all_gather.9 = f32[8,3,2048]{2,1,0:T(4,128)S(1)} all-gather(f32[1,3,2048]{2,1,0:T(4,128)S(1)} %reshape.133), channel_id=1, replica_groups=mesh['slab'=32,'hodlr'=8] {'hodlr'}, dimensions={0}, use_global_device_ids=true | all-gather | bytes 221184 | tf_op jit(solution)/shard_map/while/body/eval_jaxpr/all_gather | solution.py:83
  362.9 4.6 collective-permute-done
  373.7 13.7 %all_gather.9 = f32[8,3,2048]{2,1,0:T(4,128)S(1)} all-gather(f32[1,3,2048]{2,1,0:T(4,128)S(1)} %reshape.133), channel_id=1, replica_groups=mesh['slab'=32,'hodlr'=8] {'hodlr'}, dimensions={0}, use_global_device_ids=true | all-gather | bytes 221184 | tf_op jit(solution)/shard_map/while/body/eval_jaxpr/all_gather | solution.py:83
  392.5 4.6 collective-permute-done
  403.3 13.7 %all_gather.9 = f32[8,3,2048]{2,1,0:T(4,128)S(1)} all-gather(f32[1,3,2048]{2,1,0:T(4,128)S(1)} %reshape.133), channel_id=1, replica_groups=mesh['slab'=32,'hodlr'=8] {'hodlr'}, dimensions={0}, use_global_device_ids=true | all-gather | bytes 221184 | tf_op jit(solution)/shard_map/while/body/eval_jaxpr/all_gather | solution.py:83
  422.2 4.6 collective-permute-done
  432.9 13.7 %all_gather.9 = f32[8,3,2048]{2,1,0:T(4,128)S(1)} all-gather(f32[1,3,2048]{2,1,0:T(4,128)S(1)} %reshape.133), channel_id=1, replica_groups=mesh['slab'=32,'hodlr'=8] {'hodlr'}, dimensions={0}, use_global_device_ids=true | all-gather | bytes 221184 | tf_op jit(solution)/shard_map/while/body/eval_jaxpr/all_gather | solution.py:83
  462.6 13.7 %all_gather.9 = f32[8,3,2048]{2,1,0:T(4,128)S(1)} all-gather(f32[1,3,2048]{2,1,0:T(4,128)S(1)} %reshape.133), channel_id=1, replica_groups=mesh['slab'=32,'hodlr'=8] {'hodlr'}, dimensions={0}, use_global_device_ids=true | all-gather | bytes 221184 | tf_op jit(solution)/shard_map/while/body/eval_jaxpr/all_gather | solution.py:83
  481.4 4.6 collective-permute-done
  492.2 13.7 %all_gather.9 = f32[8,3,2048]{2,1,0:T(4,128)S(1)} all-gather(f32[1,3,2048]{2,1,0:T(4,128)S(1)} %reshape.133), channel_id=1, replica_groups=mesh['slab'=32,'hodlr'=8] {'hodlr'}, dimensions={0}, use_global_device_ids=true | all-gather | bytes 221184 | tf_op jit(solution)/shard_map/while/body/eval_jaxpr/all_gather | solution.py:83
  511.1 4.6 collective-permute-done
  521.9 13.7 %all_gather.9 = f32[8,3,2048]{2,1,0:T(4,128)S(1)} all-gather(f32[1,3,2048]{2,1,0:T(4,128)S(1)} %reshape.133), channel_id=1, replica_groups=mesh['slab'=32,'hodlr'=8] {'hodlr'}, dimensions={0}, use_global_device_ids=true | all-gather | bytes 221184 | tf_op jit(solution)/shard_map/while/body/eval_jaxpr/all_gather | solution.py:83
  540.7 4.6 collective-permute-done
  551.5 13.7 %all_gather.9 = f32[8,3,2048]{2,1,0:T(4,128)S(1)} all-gather(f32[1,3,2048]{2,1,0:T(4,128)S(1)} %reshape.133), channel_id=1, replica_groups=mesh['slab'=32,'hodlr'=8] {'hodlr'}, dimensions={0}, use_global_device_ids=true | all-gather | bytes 221184 | tf_op jit(solution)/shard_map/while/body/eval_jaxpr/all_gather | solution.py:83
  581.1 13.7 %all_gather.9 = f32[8,3,2048]{2,1,0:T(4,128)S(1)} all-gather(f32[1,3,2048]{2,1,0:T(4,128)S(1)} %reshape.133), channel_id=1, replica_groups=mesh['slab'=32,'hodlr'=8] {'hodlr'}, dimensions={0}, use_global_device_ids=true | all-gather | bytes 221184 | tf_op jit(solution)/shard_map/while/body/eval_jaxpr/all_gather | solution.py:83
  600.0 4.6 collective-permute-done
  610.8 13.7 %all_gather.9 = f32[8,3,2048]{2,1,0:T(4,128)S(1)} all-gather(f32[1,3,2048]{2,1,0:T(4,128)S(1)} %reshape.133), channel_id=1, replica_groups=mesh['slab'=32,'hodlr'=8] {'hodlr'}, dimensions={0}, use_global_device_ids=true | all-gather | bytes 221184 | tf_op jit(solution)/shard_map/while/body/eval_jaxpr/all_gather | solution.py:83
  629.6 4.6 collective-permute-done
  640.4 13.7 %all_gather.9 = f32[8,3,2048]{2,1,0:T(4,128)S(1)} all-gather(f32[1,3,2048]{2,1,0:T(4,128)S(1)} %reshape.133), channel_id=1, replica_groups=mesh['slab'=32,'hodlr'=8] {'hodlr'}, dimensions={0}, use_global_device_ids=true | all-gather | bytes 221184 | tf_op jit(solution)/shard_map/while/body/eval_jaxpr/all_gather | solution.py:83
  670.1 13.7 %all_gather.9 = f32[8,3,2048]{2,1,0:T(4,128)S(1)} all-gather(f32[1,3,2048]{2,1,0:T(4,128)S(1)} %reshape.133), channel_id=1, replica_groups=mesh['slab'=32,'hodlr'=8] {'hodlr'}, dimensions={0}, use_global_device_ids=true | all-gather | bytes 221184 | tf_op jit(solution)/shard_map/while/body/eval_jaxpr/all_gather | solution.py:83
  699.7 13.7 %all_gather.9 = f32[8,3,2048]{2,1,0:T(4,128)S(1)} all-gather(f32[1,3,2048]{2,1,0:T(4,128)S(1)} %reshape.133), channel_id=1, replica_groups=mesh['slab'=32,'hodlr'=8] {'hodlr'}, dimensions={0}, use_global_device_ids=true | all-gather | bytes 221184 | tf_op jit(solution)/shard_map/while/body/eval_jaxpr/all_gather | solution.py:83
  729.4 13.7 %all_gather.9 = f32[8,3,2048]{2,1,0:T(4,128)S(1)} all-gather(f32[1,3,2048]{2,1,0:T(4,128)S(1)} %reshape.133), channel_id=1, replica_groups=mesh['slab'=32,'hodlr'=8] {'hodlr'}, dimensions={0}, use_global_device_ids=true | all-gather | bytes 221184 | tf_op jit(solution)/shard_map/while/body/eval_jaxpr/all_gather | solution.py:83
  759.0 13.7 %all_gather.9 = f32[8,3,2048]{2,1,0:T(4,128)S(1)} all-gather(f32[1,3,2048]{2,1,0:T(4,128)S(1)} %reshape.133), channel_id=1, replica_groups=mesh['slab'=32,'hodlr'=8] {'hodlr'}, dimensions={0}, use_global_device_ids=true | all-gather | bytes 221184 | tf_op jit(solution)/shard_map/while/body/eval_jaxpr/all_gather | solution.py:83
  788.6 13.7 %all_gather.9 = f32[8,3,2048]{2,1,0:T(4,128)S(1)} all-gather(f32[1,3,2048]{2,1,0:T(4,128)S(1)} %reshape.133), channel_id=1, replica_groups=mesh['slab'=32,'hodlr'=8] {'hodlr'}, dimensions={0}, use_global_device_ids=true | all-gather | bytes 221184 | tf_op jit(solution)/shard_map/while/body/eval_jaxpr/all_gather | solution.py:83
  818.3 13.7 %all_gather.9 = f32[8,3,2048]{2,1,0:T(4,128)S(1)} all-gather(f32[1,3,2048]{2,1,0:T(4,128)S(1)} %reshape.133), channel_id=1, replica_groups=mesh['slab'=32,'hodlr'=8] {'hodlr'}, dimensions={0}, use_global_device_ids=true | all-gather | bytes 221184 | tf_op jit(solution)/shard_map/while/body/eval_jaxpr/all_gather | solution.py:83
  847.9 13.7 %all_gather.9 = f32[8,3,2048]{2,1,0:T(4,128)S(1)} all-gather(f32[1,3,2048]{2,1,0:T(4,128)S(1)} %reshape.133), channel_id=1, replica_groups=mesh['slab'=32,'hodlr'=8] {'hodlr'}, dimensions={0}, use_global_device_ids=true | all-gather | bytes 221184 | tf_op jit(solution)/shard_map/while/body/eval_jaxpr/all_gather | solution.py:83
  877.6 13.7 %all_gather.9 = f32[8,3,2048]{2,1,0:T(4,128)S(1)} all-gather(f32[1,3,2048]{2,1,0:T(4,128)S(1)} %reshape.133), channel_id=1, replica_groups=mesh['slab'=32,'hodlr'=8] {'hodlr'}, dimensions={0}, use_global_device_ids=true | all-gather | bytes 221184 | tf_op jit(solution)/shard_map/while/body/eval_jaxpr/all_gather | solution.py:83
  907.2 13.7 %all_gather.9 = f32[8,3,2048]{2,1,0:T(4,128)S(1)} all-gather(f32[1,3,2048]{2,1,0:T(4,128)S(1)} %reshape.133), channel_id=1, replica_groups=mesh['slab'=32,'hodlr'=8] {'hodlr'}, dimensions={0}, use_global_device_ids=true | all-gather | bytes 221184 | tf_op jit(solution)/shard_map/while/body/eval_jaxpr/all_gather | solution.py:83
  936.9 13.7 %all_gather.9 = f32[8,3,2048]{2,1,0:T(4,128)S(1)} all-gather(f32[1,3,2048]{2,1,0:T(4,128)S(1)} %reshape.133), channel_id=1, replica_groups=mesh['slab'=32,'hodlr'=8] {'hodlr'}, dimensions={0}, use_global_device_ids=true | all-gather | bytes 221184 | tf_op jit(solution)/shard_map/while/body/eval_jaxpr/all_gather | solution.py:83
  (664 shorter events, 439.2 us)
Async XLA Ops:
  0.1 10.9 %collective-permute-start = (bf16[32,2048]{1,0:T(8,128)(2,1)S(1)}, bf16[32,2048]{1,0:T(8,128)(2,1)S(1)}, u32[]{:S(2)}, u32[]{:S(2)}) collective-permute-start(bf16[32,2048]{1,0:T(8,128)(2,1)S(1)} %broadcast_select_fusion.2), channel_id=1, source_target_pairs={{0,8},{8,16},{16,24},{24,32},{32,40},{40,48},{48,56},{56,64},{64,7... | collective-permute-start | bytes 393224 | tf_op jit(solution)/shard_map/while/body/eval_jaxpr/ppermute | solution.py:10
  12.0 20.2 %copy-start = (bf16[4,64,2048]{2,1,0:T(8,128)(2,1)S(1)}, bf16[4,64,2048]{2,1,0:T(8,128)(2,1)}, u32[]{:S(2)}) copy-start(bf16[4,64,2048]{2,1,0:T(8,128)(2,1)} %get-tuple-element.299) | copy-start | bytes 3145732 | tf_op jit(solution)/shard_map/while
  32.5 8.9 collective-permute-start
  42.4 19.5 %copy-start = (bf16[4,64,2048]{2,1,0:T(8,128)(2,1)S(1)}, bf16[4,64,2048]{2,1,0:T(8,128)(2,1)}, u32[]{:S(2)}) copy-start(bf16[4,64,2048]{2,1,0:T(8,128)(2,1)} %get-tuple-element.299) | copy-start | bytes 3145732 | tf_op jit(solution)/shard_map/while
  62.2 8.9 collective-permute-start
  72.0 19.5 %copy-start = (bf16[4,64,2048]{2,1,0:T(8,128)(2,1)S(1)}, bf16[4,64,2048]{2,1,0:T(8,128)(2,1)}, u32[]{:S(2)}) copy-start(bf16[4,64,2048]{2,1,0:T(8,128)(2,1)} %get-tuple-element.299) | copy-start | bytes 3145732 | tf_op jit(solution)/shard_map/while
  91.8 8.9 collective-permute-start
  101.7 19.5 %copy-start = (bf16[4,64,2048]{2,1,0:T(8,128)(2,1)S(1)}, bf16[4,64,2048]{2,1,0:T(8,128)(2,1)}, u32[]{:S(2)}) copy-start(bf16[4,64,2048]{2,1,0:T(8,128)(2,1)} %get-tuple-element.299) | copy-start | bytes 3145732 | tf_op jit(solution)/shard_map/while
  121.5 8.9 collective-permute-start
  131.3 19.5 %copy-start = (bf16[4,64,2048]{2,1,0:T(8,128)(2,1)S(1)}, bf16[4,64,2048]{2,1,0:T(8,128)(2,1)}, u32[]{:S(2)}) copy-start(bf16[4,64,2048]{2,1,0:T(8,128)(2,1)} %get-tuple-element.299) | copy-start | bytes 3145732 | tf_op jit(solution)/shard_map/while
  151.1 8.9 collective-permute-start
  160.9 19.5 %copy-start = (bf16[4,64,2048]{2,1,0:T(8,128)(2,1)S(1)}, bf16[4,64,2048]{2,1,0:T(8,128)(2,1)}, u32[]{:S(2)}) copy-start(bf16[4,64,2048]{2,1,0:T(8,128)(2,1)} %get-tuple-element.299) | copy-start | bytes 3145732 | tf_op jit(solution)/shard_map/while
  180.8 8.9 collective-permute-start
  190.6 19.5 %copy-start = (bf16[4,64,2048]{2,1,0:T(8,128)(2,1)S(1)}, bf16[4,64,2048]{2,1,0:T(8,128)(2,1)}, u32[]{:S(2)}) copy-start(bf16[4,64,2048]{2,1,0:T(8,128)(2,1)} %get-tuple-element.299) | copy-start | bytes 3145732 | tf_op jit(solution)/shard_map/while
  210.4 8.9 collective-permute-start
  220.2 19.5 %copy-start = (bf16[4,64,2048]{2,1,0:T(8,128)(2,1)S(1)}, bf16[4,64,2048]{2,1,0:T(8,128)(2,1)}, u32[]{:S(2)}) copy-start(bf16[4,64,2048]{2,1,0:T(8,128)(2,1)} %get-tuple-element.299) | copy-start | bytes 3145732 | tf_op jit(solution)/shard_map/while
  240.0 8.9 collective-permute-start
  269.7 8.9 collective-permute-start
  299.3 8.9 collective-permute-start
  309.2 19.5 %copy-start = (bf16[4,64,2048]{2,1,0:T(8,128)(2,1)S(1)}, bf16[4,64,2048]{2,1,0:T(8,128)(2,1)}, u32[]{:S(2)}) copy-start(bf16[4,64,2048]{2,1,0:T(8,128)(2,1)} %get-tuple-element.299) | copy-start | bytes 3145732 | tf_op jit(solution)/shard_map/while
  329.0 8.9 collective-permute-start
  358.6 8.9 collective-permute-start
  388.3 8.9 collective-permute-start
  417.9 8.9 collective-permute-start
  427.7 19.5 %copy-start = (bf16[4,64,2048]{2,1,0:T(8,128)(2,1)S(1)}, bf16[4,64,2048]{2,1,0:T(8,128)(2,1)}, u32[]{:S(2)}) copy-start(bf16[4,64,2048]{2,1,0:T(8,128)(2,1)} %get-tuple-element.299) | copy-start | bytes 3145732 | tf_op jit(solution)/shard_map/while
  447.5 8.9 collective-permute-start
  477.2 8.9 collective-permute-start
  506.8 8.9 collective-permute-start
  516.6 19.5 %copy-start = (bf16[4,64,2048]{2,1,0:T(8,128)(2,1)S(1)}, bf16[4,64,2048]{2,1,0:T(8,128)(2,1)}, u32[]{:S(2)}) copy-start(bf16[4,64,2048]{2,1,0:T(8,128)(2,1)} %get-tuple-element.299) | copy-start | bytes 3145732 | tf_op jit(solution)/shard_map/while
  536.5 8.9 collective-permute-start
  546.3 19.5 %copy-start = (bf16[4,64,2048]{2,1,0:T(8,128)(2,1)S(1)}, bf16[4,64,2048]{2,1,0:T(8,128)(2,1)}, u32[]{:S(2)}) copy-start(bf16[4,64,2048]{2,1,0:T(8,128)(2,1)} %get-tuple-element.299) | copy-start | bytes 3145732 | tf_op jit(solution)/shard_map/while
  566.1 8.9 collective-permute-start
  595.7 8.9 collective-permute-start
  625.4 8.9 collective-permute-start
  635.2 19.5 %copy-start = (bf16[4,64,2048]{2,1,0:T(8,128)(2,1)S(1)}, bf16[4,64,2048]{2,1,0:T(8,128)(2,1)}, u32[]{:S(2)}) copy-start(bf16[4,64,2048]{2,1,0:T(8,128)(2,1)} %get-tuple-element.299) | copy-start | bytes 3145732 | tf_op jit(solution)/shard_map/while
  655.0 8.9 collective-permute-start
  664.9 19.5 %copy-start = (bf16[4,64,2048]{2,1,0:T(8,128)(2,1)S(1)}, bf16[4,64,2048]{2,1,0:T(8,128)(2,1)}, u32[]{:S(2)}) copy-start(bf16[4,64,2048]{2,1,0:T(8,128)(2,1)} %get-tuple-element.299) | copy-start | bytes 3145732 | tf_op jit(solution)/shard_map/while
  684.7 8.9 collective-permute-start
  714.3 8.9 collective-permute-start
  744.0 8.9 collective-permute-start
  753.8 19.5 %copy-start = (bf16[4,64,2048]{2,1,0:T(8,128)(2,1)S(1)}, bf16[4,64,2048]{2,1,0:T(8,128)(2,1)}, u32[]{:S(2)}) copy-start(bf16[4,64,2048]{2,1,0:T(8,128)(2,1)} %get-tuple-element.299) | copy-start | bytes 3145732 | tf_op jit(solution)/shard_map/while
  773.6 8.9 collective-permute-start
  803.2 8.9 collective-permute-start
  832.9 8.9 collective-permute-start
  862.5 8.9 collective-permute-start
  872.4 19.5 %copy-start = (bf16[4,64,2048]{2,1,0:T(8,128)(2,1)S(1)}, bf16[4,64,2048]{2,1,0:T(8,128)(2,1)}, u32[]{:S(2)}) copy-start(bf16[4,64,2048]{2,1,0:T(8,128)(2,1)} %get-tuple-element.299) | copy-start | bytes 3145732 | tf_op jit(solution)/shard_map/while
  892.2 8.9 collective-permute-start
  921.8 8.9 collective-permute-start
  (17 other events, 312.0 us)
where the time goes:
time: 958 us; the launch traced here: 952 us
  blocking collectives  439 us (46%)
  matrix products  185 us (19%)
  waiting for transfers between devices  149 us (16%)
  local copies, waits for them, and re-layouts  81.8 us (9%)
  starting transfers between devices  63.1 us (7%)
  other arithmetic  30.5 us (3%)
    all_gather x32, blocking collectives, apply(): gathered = lax.all_gather(partial_value[None], 'hodlr', axis=0, tiled=True)  439 us
    ppermute x32, waiting for transfers between devices, passed_along(): return lax.ppermute(block, axis, route)  149 us
    dot_general x32, matrix products, local_part(): jnp.einsum('sbj,bjo->sbo', w.reshape(rows, nleaf, leaf_size), leaf, prefe...  97 us
    ppermute x32, starting transfers between devices, passed_along(): return lax.ppermute(block, axis, route)  63.1 us
    dot_general x32, matrix products, partials_of(): jnp.einsum('sn,crn->csr', w, factors, preferred_element_type=jnp.float32)  52.1 us
    slice x32, local copies, waits for them, and re-layouts, local_part(): right[3].reshape(rank, block_list, block_size)  31.1 us
    slice x32, local copies, waits for them, and re-layouts, local_part(): left[3].reshape(rank, block_list, block_size)  31.1 us
    convert_element_type x32, other arithmetic, advance(): (source.astype(jnp.float32) + incoming.astype(jnp.float32)).astype(jnp.bf...  30 us
  transfers between devices with their start and end apart: 32, of which 32 were waited for; matrix products, arithmetic and copies ran while one was open for 8% of the time, Pallas kernels for 0%

commit v1 on v0

--- a/solution.py
+++ b/solution.py
@@ -1,7 +1,17 @@
+import functools
 import jax
 import jax.numpy as jnp
 from jax import lax
 from jax.sharding import PartitionSpec as P
+
+
+def refer_map_by_axis(m, on_dim):
+    return jnp.concatenate(
+        lax.all_to_all(jnp.stack([m] * lax.axis_size("hodlr")), "hodlr", 0, 0), on_dim
+    )
+
+
+direct_the_samples = functools.partial(refer_map_by_axis, on_dim=0)
 
 
 def passed_along(block, axis, distance):
@@ -80,7 +90,7 @@
         rows = w.shape[0]
         partial_value = partials_of(w, right[:cross])
         sweep_output = local_part(w)
-        gathered = lax.all_gather(partial_value[None], "hodlr", axis=0, tiled=True)
+        gathered = direct_the_samples(partial_value[None])
         sibling = combine_gathered(gathered, rows)
         return finish(sweep_output, sibling)
 

time: 958 us -> 762 us (0.80)
  blocking collectives: 439 us -> 0 us
  starting transfers between devices: 63.1 us -> 236 us
  waiting for transfers between devices: 149 us -> 193 us
  local copies, waits for them, and re-layouts: 81.8 us -> 107 us
    all_gather x32 -> x0, blocking collectives: 439 us -> none  [apply(): gathered = lax.all_gather(partial_value[None], 'hodlr', axis=0, tiled=True)]
    all_to_all x0 -> x32, starting transfers between devices: none -> 173 us  [refer_map_by_axis(): lax.all_to_all(jnp.stack([m] * lax.axis_size('hodlr')), 'hodlr', 0, 0)]
    all_to_all x0 -> x32, waiting for transfers between devices: none -> 77.1 us  [refer_map_by_axis(): lax.all_to_all(jnp.stack([m] * lax.axis_size('hodlr')), 'hodlr', 0, 0)]
    ppermute x32, waiting for transfers between devices: 149 us -> 116 us  [passed_along(): return lax.ppermute(block, axis, route)]
    another operation x0 -> x32, local copies, waits for them, and re-layouts: none -> 24.7 us  [refer_map_by_axis(): jnp.stack([m] * lax.axis_size('hodlr'))]
  transfers between devices with their start and end apart: 32 -> 64, of which waited for: 32 -> 64; matrix products, arithmetic and copies ran while one was open for 8% -> 24% of each run, Pallas kernels for 0% -> 0%
where the time goes in v1:
time: 762 us; the launch traced here: 753 us
  starting transfers between devices  236 us (31%)
  waiting for transfers between devices  193 us (25%)
  matrix products  183 us (24%)
  local copies, waits for them, and re-layouts  107 us (14%)
  other arithmetic  30.5 us (4%)
    all_to_all x32, starting transfers between devices, refer_map_by_axis(): lax.all_to_all(jnp.stack([m] * lax.axis_size('hodlr')), 'hodlr', 0, 0)  173 us
    ppermute x32, waiting for transfers between devices, passed_along(): return lax.ppermute(block, axis, route)  116 us
    dot_general x32, matrix products, local_part(): jnp.einsum('sbj,bjo->sbo', w.reshape(rows, nleaf, leaf_size), leaf, prefe...  96.3 us
    all_to_all x32, waiting for transfers between devices, refer_map_by_axis(): lax.all_to_all(jnp.stack([m] * lax.axis_size('hodlr')), 'hodlr', 0, 0)  77.1 us
    ppermute x32, starting transfers between devices, passed_along(): return lax.ppermute(block, axis, route)  63.1 us
    dot_general x32, matrix products, partials_of(): jnp.einsum('sn,crn->csr', w, factors, preferred_element_type=jnp.float32)  52.2 us
    slice x32, local copies, waits for them, and re-layouts, local_part(): left[3].reshape(rank, block_list, block_size)  31.1 us
    slice x32, local copies, waits for them, and re-layouts, local_part(): right[3].reshape(rank, block_list, block_size)  31.1 us
  transfers between devices with their start and end apart: 64, of which 64 were waited for; matrix products, arithmetic and copies ran while one was open for 24% of the time, Pallas kernels for 0%

profile of v1, /device:TPU:7, one launch (start us, length us, event | category | flops | bytes accessed | tf_op | source)
XLA Modules:
  0.0 752.6 jit_solution(3306939226200758390)
XLA Ops:
  0.1 751.9 %while.16 = (s32[]{:T(128)}, bf16[32,2048]{1,0:T(8,128)(2,1)S(1)}, bf16[32,2048]{1,0:T(8,128)(2,1)S(1)}, bf16[32,2048]{1,0:T(8,128)(2,1)}, bf16[2,1024,1024]{2,1...) while((s32[]{:T(128)}, bf16[32,2048]{1,0:T(8,128)(2,1)S(1)}, ...), condition=%wide.region_1.2_spmd.clone, body=%wide.region_0.1_spmd.clone.sunk | while | flops 202575872 | bytes 17322332 | solution.py:115
  6.0 5.1 collective-permute-done
  14.5 5.7 all-to-all-start
  31.2 3.6 collective-permute-done
  38.2 5.4 all-to-all-start
  54.6 3.6 collective-permute-done
  61.6 5.4 all-to-all-start
  78.0 3.6 collective-permute-done
  85.0 5.4 all-to-all-start
  108.4 5.4 all-to-all-start
  124.7 3.6 collective-permute-done
  131.8 5.4 all-to-all-start
  148.1 3.6 collective-permute-done
  155.1 5.4 all-to-all-start
  178.5 5.4 all-to-all-start
  201.9 5.4 all-to-all-start
  218.3 3.6 collective-permute-done
  225.3 5.4 all-to-all-start
  248.7 5.4 all-to-all-start
  272.1 5.4 all-to-all-start
  288.5 3.6 collective-permute-done
  295.5 5.4 all-to-all-start
  311.8 3.6 collective-permute-done
  318.9 5.4 all-to-all-start
  342.3 5.4 all-to-all-start
  358.6 3.6 collective-permute-done
  365.6 5.4 all-to-all-start
  382.0 3.6 collective-permute-done
  389.0 5.4 all-to-all-start
  412.4 5.4 all-to-all-start
  428.8 3.6 collective-permute-done
  435.8 5.4 all-to-all-start
  452.2 3.6 collective-permute-done
  459.2 5.4 all-to-all-start
  482.6 5.4 all-to-all-start
  499.0 3.6 collective-permute-done
  506.0 5.4 all-to-all-start
  522.4 3.6 collective-permute-done
  529.4 5.4 all-to-all-start
  552.8 5.4 all-to-all-start
  576.2 5.4 all-to-all-start
  599.5 5.4 all-to-all-start
  622.9 5.4 all-to-all-start
  646.3 5.4 all-to-all-start
  669.7 5.4 all-to-all-start
  693.1 5.4 all-to-all-start
  716.5 5.4 all-to-all-start
  739.9 5.4 all-to-all-start
  (728 shorter events, 520.8 us)
Async XLA Ops:
  0.1 10.9 %collective-permute-start = (bf16[32,2048]{1,0:T(8,128)(2,1)S(1)}, bf16[32,2048]{1,0:T(8,128)(2,1)S(1)}, u32[]{:S(2)}, u32[]{:S(2)}) collective-permute-start(bf16[32,2048]{1,0:T(8,128)(2,1)S(1)} %broadcast_select_fusion.2), channel_id=1, source_target_pairs={{0,8},{8,16},{16,24},{24,32},{32,40},{40,48},{48,56},{56,64},{64,7... | collective-permute-start | bytes 393224 | tf_op jit(solution)/shard_map/while/body/eval_jaxpr/ppermute | solution.py:20
  14.5 11.6 %all-to-all-start = ((f32[8,1,3,2048]{3,1,2,0:T(1,128)}), f32[8,1,3,2048]{3,1,2,0:T(1,128)S(1)}, u32[]{:S(2)}, u32[]{:S(2)}) async-start(f32[8,1,3,2048]{3,1,2,0:T(1,128)} %stack.19), calls=%async_computation | async-start | bytes 393216 | tf_op jit(solution)/shard_map/while/body/eval_jaxpr/all_to_all | solution.py:10
  26.9 7.8 %collective-permute-start = (bf16[32,2048]{1,0:T(8,128)(2,1)S(1)}, bf16[32,2048]{1,0:T(8,128)(2,1)S(1)}, u32[]{:S(2)}, u32[]{:S(2)}) collective-permute-start(bf16[32,2048]{1,0:T(8,128)(2,1)S(1)} %broadcast_select_fusion.2), channel_id=1, source_target_pairs={{0,8},{8,16},{16,24},{24,32},{32,40},{40,48},{48,56},{56,64},{64,7... | collective-permute-start | bytes 393224 | tf_op jit(solution)/shard_map/while/body/eval_jaxpr/ppermute | solution.py:20
  38.2 11.3 %all-to-all-start = ((f32[8,1,3,2048]{3,1,2,0:T(1,128)}), f32[8,1,3,2048]{3,1,2,0:T(1,128)S(1)}, u32[]{:S(2)}, u32[]{:S(2)}) async-start(f32[8,1,3,2048]{3,1,2,0:T(1,128)} %stack.19), calls=%async_computation | async-start | bytes 393216 | tf_op jit(solution)/shard_map/while/body/eval_jaxpr/all_to_all | solution.py:10
  50.3 7.8 %collective-permute-start = (bf16[32,2048]{1,0:T(8,128)(2,1)S(1)}, bf16[32,2048]{1,0:T(8,128)(2,1)S(1)}, u32[]{:S(2)}, u32[]{:S(2)}) collective-permute-start(bf16[32,2048]{1,0:T(8,128)(2,1)S(1)} %broadcast_select_fusion.2), channel_id=1, source_target_pairs={{0,8},{8,16},{16,24},{24,32},{32,40},{40,48},{48,56},{56,64},{64,7... | collective-permute-start | bytes 393224 | tf_op jit(solution)/shard_map/while/body/eval_jaxpr/ppermute | solution.py:20
  61.6 11.3 %all-to-all-start = ((f32[8,1,3,2048]{3,1,2,0:T(1,128)}), f32[8,1,3,2048]{3,1,2,0:T(1,128)S(1)}, u32[]{:S(2)}, u32[]{:S(2)}) async-start(f32[8,1,3,2048]{3,1,2,0:T(1,128)} %stack.19), calls=%async_computation | async-start | bytes 393216 | tf_op jit(solution)/shard_map/while/body/eval_jaxpr/all_to_all | solution.py:10
  73.7 7.8 %collective-permute-start = (bf16[32,2048]{1,0:T(8,128)(2,1)S(1)}, bf16[32,2048]{1,0:T(8,128)(2,1)S(1)}, u32[]{:S(2)}, u32[]{:S(2)}) collective-permute-start(bf16[32,2048]{1,0:T(8,128)(2,1)S(1)} %broadcast_select_fusion.2), channel_id=1, source_target_pairs={{0,8},{8,16},{16,24},{24,32},{32,40},{40,48},{48,56},{56,64},{64,7... | collective-permute-start | bytes 393224 | tf_op jit(solution)/shard_map/while/body/eval_jaxpr/ppermute | solution.py:20
  85.0 11.3 %all-to-all-start = ((f32[8,1,3,2048]{3,1,2,0:T(1,128)}), f32[8,1,3,2048]{3,1,2,0:T(1,128)S(1)}, u32[]{:S(2)}, u32[]{:S(2)}) async-start(f32[8,1,3,2048]{3,1,2,0:T(1,128)} %stack.19), calls=%async_computation | async-start | bytes 393216 | tf_op jit(solution)/shard_map/while/body/eval_jaxpr/all_to_all | solution.py:10
  97.1 7.8 %collective-permute-start = (bf16[32,2048]{1,0:T(8,128)(2,1)S(1)}, bf16[32,2048]{1,0:T(8,128)(2,1)S(1)}, u32[]{:S(2)}, u32[]{:S(2)}) collective-permute-start(bf16[32,2048]{1,0:T(8,128)(2,1)S(1)} %broadcast_select_fusion.2), channel_id=1, source_target_pairs={{0,8},{8,16},{16,24},{24,32},{32,40},{40,48},{48,56},{56,64},{64,7... | collective-permute-start | bytes 393224 | tf_op jit(solution)/shard_map/while/body/eval_jaxpr/ppermute | solution.py:20
  108.4 11.3 %all-to-all-start = ((f32[8,1,3,2048]{3,1,2,0:T(1,128)}), f32[8,1,3,2048]{3,1,2,0:T(1,128)S(1)}, u32[]{:S(2)}, u32[]{:S(2)}) async-start(f32[8,1,3,2048]{3,1,2,0:T(1,128)} %stack.19), calls=%async_computation | async-start | bytes 393216 | tf_op jit(solution)/shard_map/while/body/eval_jaxpr/all_to_all | solution.py:10
  120.5 7.8 %collective-permute-start = (bf16[32,2048]{1,0:T(8,128)(2,1)S(1)}, bf16[32,2048]{1,0:T(8,128)(2,1)S(1)}, u32[]{:S(2)}, u32[]{:S(2)}) collective-permute-start(bf16[32,2048]{1,0:T(8,128)(2,1)S(1)} %broadcast_select_fusion.2), channel_id=1, source_target_pairs={{0,8},{8,16},{16,24},{24,32},{32,40},{40,48},{48,56},{56,64},{64,7... | collective-permute-start | bytes 393224 | tf_op jit(solution)/shard_map/while/body/eval_jaxpr/ppermute | solution.py:20
  131.8 11.3 %all-to-all-start = ((f32[8,1,3,2048]{3,1,2,0:T(1,128)}), f32[8,1,3,2048]{3,1,2,0:T(1,128)S(1)}, u32[]{:S(2)}, u32[]{:S(2)}) async-start(f32[8,1,3,2048]{3,1,2,0:T(1,128)} %stack.19), calls=%async_computation | async-start | bytes 393216 | tf_op jit(solution)/shard_map/while/body/eval_jaxpr/all_to_all | solution.py:10
  143.9 7.8 %collective-permute-start = (bf16[32,2048]{1,0:T(8,128)(2,1)S(1)}, bf16[32,2048]{1,0:T(8,128)(2,1)S(1)}, u32[]{:S(2)}, u32[]{:S(2)}) collective-permute-start(bf16[32,2048]{1,0:T(8,128)(2,1)S(1)} %broadcast_select_fusion.2), channel_id=1, source_target_pairs={{0,8},{8,16},{16,24},{24,32},{32,40},{40,48},{48,56},{56,64},{64,7... | collective-permute-start | bytes 393224 | tf_op jit(solution)/shard_map/while/body/eval_jaxpr/ppermute | solution.py:20
  155.1 11.3 %all-to-all-start = ((f32[8,1,3,2048]{3,1,2,0:T(1,128)}), f32[8,1,3,2048]{3,1,2,0:T(1,128)S(1)}, u32[]{:S(2)}, u32[]{:S(2)}) async-start(f32[8,1,3,2048]{3,1,2,0:T(1,128)} %stack.19), calls=%async_computation | async-start | bytes 393216 | tf_op jit(solution)/shard_map/while/body/eval_jaxpr/all_to_all | solution.py:10
  167.3 7.8 %collective-permute-start = (bf16[32,2048]{1,0:T(8,128)(2,1)S(1)}, bf16[32,2048]{1,0:T(8,128)(2,1)S(1)}, u32[]{:S(2)}, u32[]{:S(2)}) collective-permute-start(bf16[32,2048]{1,0:T(8,128)(2,1)S(1)} %broadcast_select_fusion.2), channel_id=1, source_target_pairs={{0,8},{8,16},{16,24},{24,32},{32,40},{40,48},{48,56},{56,64},{64,7... | collective-permute-start | bytes 393224 | tf_op jit(solution)/shard_map/while/body/eval_jaxpr/ppermute | solution.py:20
  178.5 11.3 %all-to-all-start = ((f32[8,1,3,2048]{3,1,2,0:T(1,128)}), f32[8,1,3,2048]{3,1,2,0:T(1,128)S(1)}, u32[]{:S(2)}, u32[]{:S(2)}) async-start(f32[8,1,3,2048]{3,1,2,0:T(1,128)} %stack.19), calls=%async_computation | async-start | bytes 393216 | tf_op jit(solution)/shard_map/while/body/eval_jaxpr/all_to_all | solution.py:10
  190.6 7.8 %collective-permute-start = (bf16[32,2048]{1,0:T(8,128)(2,1)S(1)}, bf16[32,2048]{1,0:T(8,128)(2,1)S(1)}, u32[]{:S(2)}, u32[]{:S(2)}) collective-permute-start(bf16[32,2048]{1,0:T(8,128)(2,1)S(1)} %broadcast_select_fusion.2), channel_id=1, source_target_pairs={{0,8},{8,16},{16,24},{24,32},{32,40},{40,48},{48,56},{56,64},{64,7... | collective-permute-start | bytes 393224 | tf_op jit(solution)/shard_map/while/body/eval_jaxpr/ppermute | solution.py:20
  201.9 11.3 %all-to-all-start = ((f32[8,1,3,2048]{3,1,2,0:T(1,128)}), f32[8,1,3,2048]{3,1,2,0:T(1,128)S(1)}, u32[]{:S(2)}, u32[]{:S(2)}) async-start(f32[8,1,3,2048]{3,1,2,0:T(1,128)} %stack.19), calls=%async_computation | async-start | bytes 393216 | tf_op jit(solution)/shard_map/while/body/eval_jaxpr/all_to_all | solution.py:10
  214.0 7.8 %collective-permute-start = (bf16[32,2048]{1,0:T(8,128)(2,1)S(1)}, bf16[32,2048]{1,0:T(8,128)(2,1)S(1)}, u32[]{:S(2)}, u32[]{:S(2)}) collective-permute-start(bf16[32,2048]{1,0:T(8,128)(2,1)S(1)} %broadcast_select_fusion.2), channel_id=1, source_target_pairs={{0,8},{8,16},{16,24},{24,32},{32,40},{40,48},{48,56},{56,64},{64,7... | collective-permute-start | bytes 393224 | tf_op jit(solution)/shard_map/while/body/eval_jaxpr/ppermute | solution.py:20
  225.3 11.3 %all-to-all-start = ((f32[8,1,3,2048]{3,1,2,0:T(1,128)}), f32[8,1,3,2048]{3,1,2,0:T(1,128)S(1)}, u32[]{:S(2)}, u32[]{:S(2)}) async-start(f32[8,1,3,2048]{3,1,2,0:T(1,128)} %stack.19), calls=%async_computation | async-start | bytes 393216 | tf_op jit(solution)/shard_map/while/body/eval_jaxpr/all_to_all | solution.py:10
  248.7 11.3 %all-to-all-start = ((f32[8,1,3,2048]{3,1,2,0:T(1,128)}), f32[8,1,3,2048]{3,1,2,0:T(1,128)S(1)}, u32[]{:S(2)}, u32[]{:S(2)}) async-start(f32[8,1,3,2048]{3,1,2,0:T(1,128)} %stack.19), calls=%async_computation | async-start | bytes 393216 | tf_op jit(solution)/shard_map/while/body/eval_jaxpr/all_to_all | solution.py:10
  260.8 7.8 %collective-permute-start = (bf16[32,2048]{1,0:T(8,128)(2,1)S(1)}, bf16[32,2048]{1,0:T(8,128)(2,1)S(1)}, u32[]{:S(2)}, u32[]{:S(2)}) collective-permute-start(bf16[32,2048]{1,0:T(8,128)(2,1)S(1)} %broadcast_select_fusion.2), channel_id=1, source_target_pairs={{0,8},{8,16},{16,24},{24,32},{32,40},{40,48},{48,56},{56,64},{64,7... | collective-permute-start | bytes 393224 | tf_op jit(solution)/shard_map/while/body/eval_jaxpr/ppermute | solution.py:20
  272.1 11.3 %all-to-all-start = ((f32[8,1,3,2048]{3,1,2,0:T(1,128)}), f32[8,1,3,2048]{3,1,2,0:T(1,128)S(1)}, u32[]{:S(2)}, u32[]{:S(2)}) async-start(f32[8,1,3,2048]{3,1,2,0:T(1,128)} %stack.19), calls=%async_computation | async-start | bytes 393216 | tf_op jit(solution)/shard_map/while/body/eval_jaxpr/all_to_all | solution.py:10
  284.2 7.8 %collective-permute-start = (bf16[32,2048]{1,0:T(8,128)(2,1)S(1)}, bf16[32,2048]{1,0:T(8,128)(2,1)S(1)}, u32[]{:S(2)}, u32[]{:S(2)}) collective-permute-start(bf16[32,2048]{1,0:T(8,128)(2,1)S(1)} %broadcast_select_fusion.2), channel_id=1, source_target_pairs={{0,8},{8,16},{16,24},{24,32},{32,40},{40,48},{48,56},{56,64},{64,7... | collective-permute-start | bytes 393224 | tf_op jit(solution)/shard_map/while/body/eval_jaxpr/ppermute | solution.py:20
  295.5 11.3 %all-to-all-start = ((f32[8,1,3,2048]{3,1,2,0:T(1,128)}), f32[8,1,3,2048]{3,1,2,0:T(1,128)S(1)}, u32[]{:S(2)}, u32[]{:S(2)}) async-start(f32[8,1,3,2048]{3,1,2,0:T(1,128)} %stack.19), calls=%async_computation | async-start | bytes 393216 | tf_op jit(solution)/shard_map/while/body/eval_jaxpr/all_to_all | solution.py:10
  307.6 7.8 %collective-permute-start = (bf16[32,2048]{1,0:T(8,128)(2,1)S(1)}, bf16[32,2048]{1,0:T(8,128)(2,1)S(1)}, u32[]{:S(2)}, u32[]{:S(2)}) collective-permute-start(bf16[32,2048]{1,0:T(8,128)(2,1)S(1)} %broadcast_select_fusion.2), channel_id=1, source_target_pairs={{0,8},{8,16},{16,24},{24,32},{32,40},{40,48},{48,56},{56,64},{64,7... | collective-permute-start | bytes 393224 | tf_op jit(solution)/shard_map/while/body/eval_jaxpr/ppermute | solution.py:20
  318.9 11.3 %all-to-all-start = ((f32[8,1,3,2048]{3,1,2,0:T(1,128)}), f32[8,1,3,2048]{3,1,2,0:T(1,128)S(1)}, u32[]{:S(2)}, u32[]{:S(2)}) async-start(f32[8,1,3,2048]{3,1,2,0:T(1,128)} %stack.19), calls=%async_computation | async-start | bytes 393216 | tf_op jit(solution)/shard_map/while/body/eval_jaxpr/all_to_all | solution.py:10
  331.0 7.8 %collective-permute-start = (bf16[32,2048]{1,0:T(8,128)(2,1)S(1)}, bf16[32,2048]{1,0:T(8,128)(2,1)S(1)}, u32[]{:S(2)}, u32[]{:S(2)}) collective-permute-start(bf16[32,2048]{1,0:T(8,128)(2,1)S(1)} %broadcast_select_fusion.2), channel_id=1, source_target_pairs={{0,8},{8,16},{16,24},{24,32},{32,40},{40,48},{48,56},{56,64},{64,7... | collective-permute-start | bytes 393224 | tf_op jit(solution)/shard_map/while/body/eval_jaxpr/ppermute | solution.py:20
  342.3 11.3 %all-to-all-start = ((f32[8,1,3,2048]{3,1,2,0:T(1,128)}), f32[8,1,3,2048]{3,1,2,0:T(1,128)S(1)}, u32[]{:S(2)}, u32[]{:S(2)}) async-start(f32[8,1,3,2048]{3,1,2,0:T(1,128)} %stack.19), calls=%async_computation | async-start | bytes 393216 | tf_op jit(solution)/shard_map/while/body/eval_jaxpr/all_to_all | solution.py:10
  354.4 7.8 %collective-permute-start = (bf16[32,2048]{1,0:T(8,128)(2,1)S(1)}, bf16[32,2048]{1,0:T(8,128)(2,1)S(1)}, u32[]{:S(2)}, u32[]{:S(2)}) collective-permute-start(bf16[32,2048]{1,0:T(8,128)(2,1)S(1)} %broadcast_select_fusion.2), channel_id=1, source_target_pairs={{0,8},{8,16},{16,24},{24,32},{32,40},{40,48},{48,56},{56,64},{64,7... | collective-permute-start | bytes 393224 | tf_op jit(solution)/shard_map/while/body/eval_jaxpr/ppermute | solution.py:20
  365.6 11.3 %all-to-all-start = ((f32[8,1,3,2048]{3,1,2,0:T(1,128)}), f32[8,1,3,2048]{3,1,2,0:T(1,128)S(1)}, u32[]{:S(2)}, u32[]{:S(2)}) async-start(f32[8,1,3,2048]{3,1,2,0:T(1,128)} %stack.19), calls=%async_computation | async-start | bytes 393216 | tf_op jit(solution)/shard_map/while/body/eval_jaxpr/all_to_all | solution.py:10
  377.8 7.8 %collective-permute-start = (bf16[32,2048]{1,0:T(8,128)(2,1)S(1)}, bf16[32,2048]{1,0:T(8,128)(2,1)S(1)}, u32[]{:S(2)}, u32[]{:S(2)}) collective-permute-start(bf16[32,2048]{1,0:T(8,128)(2,1)S(1)} %broadcast_select_fusion.2), channel_id=1, source_target_pairs={{0,8},{8,16},{16,24},{24,32},{32,40},{40,48},{48,56},{56,64},{64,7... | collective-permute-start | bytes 393224 | tf_op jit(solution)/shard_map/while/body/eval_jaxpr/ppermute | solution.py:20
  389.0 11.3 %all-to-all-start = ((f32[8,1,3,2048]{3,1,2,0:T(1,128)}), f32[8,1,3,2048]{3,1,2,0:T(1,128)S(1)}, u32[]{:S(2)}, u32[]{:S(2)}) async-start(f32[8,1,3,2048]{3,1,2,0:T(1,128)} %stack.19), calls=%async_computation | async-start | bytes 393216 | tf_op jit(solution)/shard_map/while/body/eval_jaxpr/all_to_all | solution.py:10
  412.4 11.3 %all-to-all-start = ((f32[8,1,3,2048]{3,1,2,0:T(1,128)}), f32[8,1,3,2048]{3,1,2,0:T(1,128)S(1)}, u32[]{:S(2)}, u32[]{:S(2)}) async-start(f32[8,1,3,2048]{3,1,2,0:T(1,128)} %stack.19), calls=%async_computation | async-start | bytes 393216 | tf_op jit(solution)/shard_map/while/body/eval_jaxpr/all_to_all | solution.py:10
  435.8 11.3 %all-to-all-start = ((f32[8,1,3,2048]{3,1,2,0:T(1,128)}), f32[8,1,3,2048]{3,1,2,0:T(1,128)S(1)}, u32[]{:S(2)}, u32[]{:S(2)}) async-start(f32[8,1,3,2048]{3,1,2,0:T(1,128)} %stack.19), calls=%async_computation | async-start | bytes 393216 | tf_op jit(solution)/shard_map/while/body/eval_jaxpr/all_to_all | solution.py:10
  459.2 11.3 %all-to-all-start = ((f32[8,1,3,2048]{3,1,2,0:T(1,128)}), f32[8,1,3,2048]{3,1,2,0:T(1,128)S(1)}, u32[]{:S(2)}, u32[]{:S(2)}) async-start(f32[8,1,3,2048]{3,1,2,0:T(1,128)} %stack.19), calls=%async_computation | async-start | bytes 393216 | tf_op jit(solution)/shard_map/while/body/eval_jaxpr/all_to_all | solution.py:10
  482.6 11.3 %all-to-all-start = ((f32[8,1,3,2048]{3,1,2,0:T(1,128)}), f32[8,1,3,2048]{3,1,2,0:T(1,128)S(1)}, u32[]{:S(2)}, u32[]{:S(2)}) async-start(f32[8,1,3,2048]{3,1,2,0:T(1,128)} %stack.19), calls=%async_computation | async-start | bytes 393216 | tf_op jit(solution)/shard_map/while/body/eval_jaxpr/all_to_all | solution.py:10
  506.0 11.3 %all-to-all-start = ((f32[8,1,3,2048]{3,1,2,0:T(1,128)}), f32[8,1,3,2048]{3,1,2,0:T(1,128)S(1)}, u32[]{:S(2)}, u32[]{:S(2)}) async-start(f32[8,1,3,2048]{3,1,2,0:T(1,128)} %stack.19), calls=%async_computation | async-start | bytes 393216 | tf_op jit(solution)/shard_map/while/body/eval_jaxpr/all_to_all | solution.py:10
  529.4 11.3 %all-to-all-start = ((f32[8,1,3,2048]{3,1,2,0:T(1,128)}), f32[8,1,3,2048]{3,1,2,0:T(1,128)S(1)}, u32[]{:S(2)}, u32[]{:S(2)}) async-start(f32[8,1,3,2048]{3,1,2,0:T(1,128)} %stack.19), calls=%async_computation | async-start | bytes 393216 | tf_op jit(solution)/shard_map/while/body/eval_jaxpr/all_to_all | solution.py:10
  552.8 11.3 %all-to-all-start = ((f32[8,1,3,2048]{3,1,2,0:T(1,128)}), f32[8,1,3,2048]{3,1,2,0:T(1,128)S(1)}, u32[]{:S(2)}, u32[]{:S(2)}) async-start(f32[8,1,3,2048]{3,1,2,0:T(1,128)} %stack.19), calls=%async_computation | async-start | bytes 393216 | tf_op jit(solution)/shard_map/while/body/eval_jaxpr/all_to_all | solution.py:10
  576.2 11.3 %all-to-all-start = ((f32[8,1,3,2048]{3,1,2,0:T(1,128)}), f32[8,1,3,2048]{3,1,2,0:T(1,128)S(1)}, u32[]{:S(2)}, u32[]{:S(2)}) async-start(f32[8,1,3,2048]{3,1,2,0:T(1,128)} %stack.19), calls=%async_computation | async-start | bytes 393216 | tf_op jit(solution)/shard_map/while/body/eval_jaxpr/all_to_all | solution.py:10
  599.5 11.3 %all-to-all-start = ((f32[8,1,3,2048]{3,1,2,0:T(1,128)}), f32[8,1,3,2048]{3,1,2,0:T(1,128)S(1)}, u32[]{:S(2)}, u32[]{:S(2)}) async-start(f32[8,1,3,2048]{3,1,2,0:T(1,128)} %stack.19), calls=%async_computation | async-start | bytes 393216 | tf_op jit(solution)/shard_map/while/body/eval_jaxpr/all_to_all | solution.py:10
  622.9 11.3 %all-to-all-start = ((f32[8,1,3,2048]{3,1,2,0:T(1,128)}), f32[8,1,3,2048]{3,1,2,0:T(1,128)S(1)}, u32[]{:S(2)}, u32[]{:S(2)}) async-start(f32[8,1,3,2048]{3,1,2,0:T(1,128)} %stack.19), calls=%async_computation | async-start | bytes 393216 | tf_op jit(solution)/shard_map/while/body/eval_jaxpr/all_to_all | solution.py:10
  646.3 11.3 %all-to-all-start = ((f32[8,1,3,2048]{3,1,2,0:T(1,128)}), f32[8,1,3,2048]{3,1,2,0:T(1,128)S(1)}, u32[]{:S(2)}, u32[]{:S(2)}) async-start(f32[8,1,3,2048]{3,1,2,0:T(1,128)} %stack.19), calls=%async_computation | async-start | bytes 393216 | tf_op jit(solution)/shard_map/while/body/eval_jaxpr/all_to_all | solution.py:10
  669.7 11.3 %all-to-all-start = ((f32[8,1,3,2048]{3,1,2,0:T(1,128)}), f32[8,1,3,2048]{3,1,2,0:T(1,128)S(1)}, u32[]{:S(2)}, u32[]{:S(2)}) async-start(f32[8,1,3,2048]{3,1,2,0:T(1,128)} %stack.19), calls=%async_computation | async-start | bytes 393216 | tf_op jit(solution)/shard_map/while/body/eval_jaxpr/all_to_all | solution.py:10
  693.1 11.3 %all-to-all-start = ((f32[8,1,3,2048]{3,1,2,0:T(1,128)}), f32[8,1,3,2048]{3,1,2,0:T(1,128)S(1)}, u32[]{:S(2)}, u32[]{:S(2)}) async-start(f32[8,1,3,2048]{3,1,2,0:T(1,128)} %stack.19), calls=%async_computation | async-start | bytes 393216 | tf_op jit(solution)/shard_map/while/body/eval_jaxpr/all_to_all | solution.py:10
  716.5 11.3 %all-to-all-start = ((f32[8,1,3,2048]{3,1,2,0:T(1,128)}), f32[8,1,3,2048]{3,1,2,0:T(1,128)S(1)}, u32[]{:S(2)}, u32[]{:S(2)}) async-start(f32[8,1,3,2048]{3,1,2,0:T(1,128)} %stack.19), calls=%async_computation | async-start | bytes 393216 | tf_op jit(solution)/shard_map/while/body/eval_jaxpr/all_to_all | solution.py:10
  739.9 11.3 %all-to-all-start = ((f32[8,1,3,2048]{3,1,2,0:T(1,128)}), f32[8,1,3,2048]{3,1,2,0:T(1,128)S(1)}, u32[]{:S(2)}, u32[]{:S(2)}) async-start(f32[8,1,3,2048]{3,1,2,0:T(1,128)} %stack.19), calls=%async_computation | async-start | bytes 393216 | tf_op jit(solution)/shard_map/while/body/eval_jaxpr/all_to_all | solution.py:10
  (49 other events, 582.9 us)
